TPU v7x, 512 devices: a whole 4x8x8 slice. The times are simulated.
512 devices in a mesh: tm: 16 (over z, core), lat: 32 (over x, y).
Axes of the slice: x: 4, y: 8, z: 8, core: 2. Of those that a mesh axis runs over, the one named last changes fastest.
Arguments:
- trajectory: float32 [16, 84, 128, 128], P('tm', None, 'lat'), may hold values from -6 to 6
- step_levels: int32 [17], replicated, may hold values from 0 to 63, as said below
- in_weight: bfloat16 [256, 84], replicated, may hold values from -0.625 to 0.625
- in_bias: float32 [256], replicated, may hold values from -4 to 4
- conv_weight: bfloat16 [2, 256, 2304], replicated, may hold values from -0.125 to 0.125
- cond_weight: bfloat16 [256, 1024], replicated, may hold values from -0.375 to 0.375
- out_weight: bfloat16 [84, 256], replicated, may hold values from -0.375 to 0.375
Outputs:
- advanced: float32 [16, 84, 128, 128], P('tm', None, 'lat')
Inputs may be any that keep to these rules, and one draw needn't show every extreme that they name: `step_levels`: strictly increasing; the first entry is 0 and the last is 63.
All inputs are finite; a program needn't handle non-finite values.
Results may differ from a plain program's by a relative error of at most 0.0055.
Values may be sent and summed in bfloat16 or wider, within the bound.
No kernel may reach another device: no remote copies, remote signals or barrier semaphores. Data moves between devices by JAX's collectives and lax.ppermute only.
A program may use at most 64 MiB of HBM per device.

v0:
```python
import jax
import jax.numpy as jnp
from jax import lax
from jax.sharding import PartitionSpec as P

LEVELS = 64
ITERS = 2
sigma_top = 1.0
sigma_low = 0.02
rho_power = 7.0


def extended(block, sides, width):
    for axis, dim in sides:
        count = lax.axis_size(axis)
        forward = [(i, i + 1) for i in range(count - 1)]
        backward = [(target, source) for source, target in forward]
        low = lax.ppermute(
            lax.slice_in_dim(block, block.shape[dim] - width, None, axis=dim), axis, forward
        )
        high = lax.ppermute(lax.slice_in_dim(block, 0, width, axis=dim), axis, backward)
        block = jnp.concatenate([low, block, high], axis=dim)
    return block


def carried_in(value, axis, join, neutral):
    count, mine = (lax.axis_size(axis), lax.axis_index(axis))
    pieces = lax.all_gather(value, axis)
    subtotal = jnp.full_like(value, 0) + jnp.asarray(neutral, value.dtype)

    def hop(position, subtotal):
        longer = join(subtotal, pieces[position])
        return jnp.where(position < mine, longer, subtotal)

    return lax.fori_loop(0, count - 1, hop, subtotal)


def from_root(array, axis, root):
    mine = lax.axis_index(axis) == root
    return lax.psum(jnp.where(mine, array, jnp.zeros_like(array)), axis)


def level_sigma(levels):
    fraction = levels.astype(jnp.float32) / (LEVELS - 1)
    root_value = sigma_top ** (1.0 / rho_power) + fraction * (
        sigma_low ** (1.0 / rho_power) - sigma_top ** (1.0 / rho_power)
    )
    return root_value**rho_power


def conditions_of(sigma_now, cond_weight):
    freq_count = cond_weight.shape[0] // 2
    frequency = 100.0 ** (jnp.arange(freq_count).astype(jnp.float32) / freq_count)
    phases = jnp.log(sigma_now) / 4.0 * frequency
    embedding = jnp.concatenate([jnp.cos(phases), jnp.sin(phases)]).astype(jnp.bfloat16)[None, :]
    conditions = jnp.dot(embedding, cond_weight, preferred_element_type=jnp.float32)[0]
    return jnp.split(conditions, 4)


def convolve(padded, weight):
    row_count = padded.shape[1] - 2
    shifted = []
    for offset_row in range(3):
        for offset_col in (-1, 0, 1):
            shifted.append(
                jnp.roll(padded[:, offset_row : offset_row + row_count, :], -offset_col, axis=2)
            )
    columns_all = jnp.concatenate(shifted, axis=0)
    flattened = columns_all.reshape(columns_all.shape[0], -1)
    response = jnp.dot(weight, flattened, preferred_element_type=jnp.float32)
    return response.reshape(weight.shape[0], row_count, padded.shape[2])


def project(scaled, in_weight, in_bias):
    channels, row_count, columns = scaled.shape
    hidden = (
        jnp.dot(in_weight, scaled.reshape(channels, -1), preferred_element_type=jnp.float32)
        + in_bias[:, None]
    )
    return hidden.reshape(-1, row_count, columns)


def field_drift(
    current, sigma_now, sigma_next, in_weight, in_bias, conv_weight, cond_weight, out_weight
):
    scale_one, shift_one, scale_two, shift_two = conditions_of(sigma_now, cond_weight)
    variance = sigma_now * sigma_now + 0.25
    scaled = (current / jnp.sqrt(variance)).astype(jnp.bfloat16)
    channels, row_count, columns = current.shape
    hidden_zero = project(scaled, in_weight, in_bias).astype(jnp.bfloat16)
    padded = extended(hidden_zero, (("lat", 1),), 1)
    response = convolve(padded, conv_weight[0])
    hidden_one = jax.nn.silu(
        response * (1.0 + scale_one[:, None, None]) + shift_one[:, None, None]
    ).astype(jnp.bfloat16)
    padded_one = extended(hidden_one, (("lat", 1),), 1)
    response = convolve(padded_one, conv_weight[1])
    hidden_two = hidden_one.astype(jnp.float32) + jax.nn.silu(
        response * (1.0 + scale_two[:, None, None]) + shift_two[:, None, None]
    )
    hidden_two = hidden_two.astype(jnp.bfloat16)
    network = jnp.dot(
        out_weight, hidden_two.reshape(hidden_two.shape[0], -1), preferred_element_type=jnp.float32
    )
    network = network.reshape(channels, row_count, columns)
    denoised = 0.25 / variance * current + 0.5 * sigma_now / jnp.sqrt(variance) * network
    return (current - denoised) * ((sigma_next - sigma_now) / sigma_now)


def add_pair(earlier_sum, later_sum):
    return earlier_sum + later_sum


def earlier_drifts(carried):
    return carried_in(carried, "tm", add_pair, jnp.zeros_like(carried))


def on_device(trajectory, step_levels, in_weight, in_bias, conv_weight, cond_weight, out_weight):
    time_slot = lax.axis_index("tm")
    current = trajectory[0]
    bounds = lax.dynamic_slice_in_dim(step_levels, time_slot, 2)
    sigmas = level_sigma(bounds)
    sigma_now = sigmas[0]
    sigma_next = sigmas[1]
    anchor = from_root(current, "tm", 0)
    result = current
    for sweep in range(ITERS):
        drift_term = field_drift(
            current, sigma_now, sigma_next, in_weight, in_bias, conv_weight, cond_weight, out_weight
        )
        earlier = earlier_drifts(drift_term)
        if sweep + 1 < ITERS:
            current = earlier + anchor
        else:
            result = earlier + anchor + drift_term
    return result[None]


def solution(mesh):
    in_specs = (P("tm", None, "lat", None), P(), P(), P(), P(), P(), P())
    out_specs = P("tm", None, "lat", None)
    return jax.shard_map(
        on_device, mesh=mesh, in_specs=in_specs, out_specs=out_specs, check_vma=False
    )
```

profile of v0, /device:TPU:1, one launch (start us, length us, event | category | flops | bytes accessed | tf_op | source)
XLA Modules:
  0.0 298.3 jit_solution(8111973741452247749)
XLA Ops:
  9.3 1.6 select_bitcast_fusion
  12.1 4.0 %collective-permute-start = (bf16[256,1,128]{0,2,1:T(8,128)(2,1)S(1)}, bf16[256,1,128]{0,2,1:T(8,128)(2,1)S(1)}, u32[]{:S(2)}, u32[]{:S(2)}) collective-permute-start(bf16[256,1,128]{0,2,1:T(8,128)(2,1)S(1)} %get-tuple-element.258), channel_id=1, source_target_pairs={{0,1},{1,2},{2,3},{3,4},{4,5},{5,6},{6,7},{7,8},{8,9},{9,10},{10,1... | collective-permute-start | bytes 196616 | tf_op jit(solution)/shard_map/ppermute | solution.py:18
  16.1 1.3 collective-permute-start.1
  21.9 1.4 copy-done.8
  24.2 4.0 %collective-permute-start.2 = (bf16[256,1,128]{0,2,1:T(8,128)(2,1)S(1)}, bf16[256,1,128]{0,2,1:T(8,128)(2,1)S(1)}, u32[]{:S(2)}, u32[]{:S(2)}) collective-permute-start(bf16[256,1,128]{0,2,1:T(8,128)(2,1)S(1)} %get-tuple-element.250), channel_id=1, source_target_pairs={{0,1},{1,2},{2,3},{3,4},{4,5},{5,6},{6,7},{7,8},{8,9},{9,10},{10,1... | collective-permute-start | bytes 196616 | tf_op jit(solution)/shard_map/ppermute | solution.py:18
  28.2 1.3 collective-permute-start.3
  29.5 3.7 %collective-permute-done.3 = bf16[256,1,128]{0,2,1:T(8,128)(2,1)S(1)} collective-permute-done((bf16[256,1,128]{0,2,1:T(8,128)(2,1)S(1)}, bf16[256,1,128]{0,2,1:T(8,128)(2,1)S(1)}, u32[]{:S(2)}, u32[]{:S(2)}) %collective-permute-start.3) | collective-permute-done | bytes 65568 | tf_op jit(solution)/shard_map/ppermute | solution.py:21
  34.0 1.4 copy-done.5
  35.4 3.2 %fusion.13 = f32[84,512]{1,0:T(8,128)S(1)} fusion(bf16[84,256]{1,0:T(8,128)(2,1)S(1)} %copy-done.10, bf16[2304,512]{0,1:T(8,128)(2,1)} %bitcast.145, bf16[2,256,2304]{2,1,0:T(8,128)(2,1)} %param.15, f32[512,256]{1,0:T(8,128)S(1)} %fusion.10, f32[256]{0:T(256)S(1)} %get-tuple-element.264, f32[256]{0:T(256)S(1)} %get-tuple-element.263, ...), kind=kOutput, calls=%fused_computation.21 | convolution fusion | flops 628140032 | bytes 4282372 | tf_op jit(solution)/shard_map/dot_general | solution.py:102
  40.3 51.2 %all-gather.4.cloned.1.call-done = f32[16,84,4,128]{3,2,1,0:T(4,128)} async-done(((f32[1,84,4,128]{3,2,1,0:T(4,128)}), f32[16,84,4,128]{3,2,1,0:T(4,128)}) %all-gather.4.cloned.1.call-update) | async-done | bytes 2752528 | tf_op jit(solution)/shard_map/all_gather | solution.py:28
  91.5 17.4 %while.28 = (s32[]{:T(128)}, f32[84,4,128]{2,1,0:T(4,128)S(1)}, s32[]{:T(128)}, f32[16,84,4,128]{3,2,1,0:T(4,128)}, s32[]{:T(128)}, /*index=5*/s32[]{:T(128)}) while((s32[]{:T(128)}, f32[84,4,128]{2,1,0:T(4,128)S(1)}, s32[]{:T(128)}, f32[16,84,4,128]{3,2,1,0:T(4,128)}, s32[]{:T(128)}, /*index=5*/s32[]{:T(128)}) %tuple.98), condition=%wide.region_1.2_spmd.clone, body=%wide.region_0.1_spmd.clone.sunk | while | flops 129028 | bytes 516189 | solution.py:35
  92.7 1.1 add_select_fusion.4
  93.8 1.1 add_select_fusion.4
  95.0 1.1 add_select_fusion.4
  96.1 1.1 add_select_fusion.4
  97.3 1.1 add_select_fusion.4
  98.4 1.1 add_select_fusion.4
  99.6 1.1 add_select_fusion.4
  100.8 1.1 add_select_fusion.4
  101.9 1.1 add_select_fusion.4
  103.1 1.1 add_select_fusion.4
  104.2 1.1 add_select_fusion.4
  105.4 1.1 add_select_fusion.4
  106.5 1.1 add_select_fusion.4
  107.7 1.1 add_select_fusion.4
  108.9 92.6 %all-reduce.2.cloned.1.call-done = f32[84,4,128]{2,1,0:T(4,128)} async-done(((f32[84,4,128]{2,1,0:T(4,128)}), f32[84,4,128]{2,1,0:T(4,128)}) %all-reduce.2.cloned.1.call-update) | async-done | bytes 172048 | tf_op jit(solution)/shard_map/psum | solution.py:40
  202.8 3.1 %collective-permute-start.4 = (bf16[256,1,128]{0,2,1:T(8,128)(2,1)S(1)}, bf16[256,1,128]{0,2,1:T(8,128)(2,1)S(1)}, u32[]{:S(2)}, u32[]{:S(2)}) collective-permute-start(bf16[256,1,128]{0,2,1:T(8,128)(2,1)S(1)} %get-tuple-element.242), channel_id=1, source_target_pairs={{0,1},{1,2},{2,3},{3,4},{4,5},{5,6},{6,7},{7,8},{8,9},{9,10},{10,1... | collective-permute-start | bytes 196616 | tf_op jit(solution)/shard_map/ppermute | solution.py:18
  206.0 1.3 collective-permute-start.5
  207.5 3.8 %collective-permute-done.5 = bf16[256,1,128]{0,2,1:T(8,128)(2,1)S(1)} collective-permute-done((bf16[256,1,128]{0,2,1:T(8,128)(2,1)S(1)}, bf16[256,1,128]{0,2,1:T(8,128)(2,1)S(1)}, u32[]{:S(2)}, u32[]{:S(2)}) %collective-permute-start.5) | collective-permute-done | bytes 65568 | tf_op jit(solution)/shard_map/ppermute | solution.py:21
  212.0 1.4 copy-done.9
  214.4 3.1 %collective-permute-start.6 = (bf16[256,1,128]{0,2,1:T(8,128)(2,1)S(1)}, bf16[256,1,128]{0,2,1:T(8,128)(2,1)S(1)}, u32[]{:S(2)}, u32[]{:S(2)}) collective-permute-start(bf16[256,1,128]{0,2,1:T(8,128)(2,1)S(1)} %get-tuple-element.234), channel_id=1, source_target_pairs={{0,1},{1,2},{2,3},{3,4},{4,5},{5,6},{6,7},{7,8},{8,9},{9,10},{10,1... | collective-permute-start | bytes 196616 | tf_op jit(solution)/shard_map/ppermute | solution.py:18
  217.5 1.3 collective-permute-start.7
  218.8 4.7 %collective-permute-done.7 = bf16[256,1,128]{0,2,1:T(8,128)(2,1)S(1)} collective-permute-done((bf16[256,1,128]{0,2,1:T(8,128)(2,1)S(1)}, bf16[256,1,128]{0,2,1:T(8,128)(2,1)S(1)}, u32[]{:S(2)}, u32[]{:S(2)}) %collective-permute-start.7) | collective-permute-done | bytes 65568 | tf_op jit(solution)/shard_map/ppermute | solution.py:21
  224.3 1.4 copy-done.6
  225.7 3.1 %fusion.12 = f32[84,512]{1,0:T(8,128)S(1)} fusion(bf16[84,256]{1,0:T(8,128)(2,1)S(1)} %copy-done.10, bf16[2304,512]{0,1:T(8,128)(2,1)} %bitcast.147, bf16[2,256,2304]{2,1,0:T(8,128)(2,1)} %param.15, f32[512,256]{1,0:T(8,128)S(1)} %fusion.8, f32[256]{0:T(256)S(1)} %get-tuple-element.264, f32[256]{0:T(256)S(1)} %get-tuple-element.263, ...), kind=kOutput, calls=%fused_computation.19 | convolution fusion | flops 628140032 | bytes 4282372 | tf_op jit(solution)/shard_map/dot_general | solution.py:102
  229.6 44.0 %all-gather.6.cloned.1.call-done = f32[1344,4,128]{2,1,0:T(4,128)} async-done(((f32[84,4,128]{2,1,0:T(4,128)}), f32[1344,4,128]{2,1,0:T(4,128)}) %all-gather.6.cloned.1.call-update) | async-done | bytes 2752528 | tf_op jit(solution)/shard_map/all_gather | solution.py:28
  273.7 17.3 %while.29 = (s32[]{:T(128)}, f32[84,4,128]{2,1,0:T(4,128)S(1)}, s32[]{:T(128)}, f32[16,84,4,128]{3,2,1,0:T(4,128)}, s32[]{:T(128)}, /*index=5*/s32[]{:T(128)}) while((s32[]{:T(128)}, f32[84,4,128]{2,1,0:T(4,128)S(1)}, s32[]{:T(128)}, f32[16,84,4,128]{3,2,1,0:T(4,128)}, s32[]{:T(128)}, /*index=5*/s32[]{:T(128)}) %tuple.110), condition=%wide.region_4.5_spmd.clone, body=%wide.region_3.4_spmd.clone.sunk | while | flops 129028 | bytes 516189 | solution.py:35
  274.8 1.1 add_select_fusion.5
  276.0 1.1 add_select_fusion.5
  277.1 1.1 add_select_fusion.5
  278.3 1.1 add_select_fusion.5
  279.4 1.1 add_select_fusion.5
  280.6 1.1 add_select_fusion.5
  281.8 1.1 add_select_fusion.5
  282.9 1.1 add_select_fusion.5
  284.1 1.1 add_select_fusion.5
  285.2 1.1 add_select_fusion.5
  286.4 1.1 add_select_fusion.5
  (107 shorter events, 17.6 us)
Async XLA Ops:
  6.5 11.7 %copy-start = (bf16[256,1024]{1,0:T(8,128)(2,1)S(1)}, bf16[256,1024]{1,0:T(8,128)(2,1)}, u32[]{:S(2)}) copy-start(bf16[256,1024]{1,0:T(8,128)(2,1)} %param.16) | copy-start | bytes 1572868
  6.5 85.0 %all-gather.4.cloned.1.call-start = ((), (), s32[]{:S(2)}) async-start(), calls=%async_computation | async-start | bytes 2924544 | tf_op jit(solution)/shard_map/all_gather | solution.py:28
  12.1 9.1 %collective-permute-start = (bf16[256,1,128]{0,2,1:T(8,128)(2,1)S(1)}, bf16[256,1,128]{0,2,1:T(8,128)(2,1)S(1)}, u32[]{:S(2)}, u32[]{:S(2)}) collective-permute-start(bf16[256,1,128]{0,2,1:T(8,128)(2,1)S(1)} %get-tuple-element.258), channel_id=1, source_target_pairs={{0,1},{1,2},{2,3},{3,4},{4,5},{5,6},{6,7},{7,8},{8,9},{9,10},{10,1... | collective-permute-start | bytes 196616 | tf_op jit(solution)/shard_map/ppermute | solution.py:18
  16.1 5.1 %collective-permute-start.1 = (bf16[256,1,128]{0,2,1:T(8,128)(2,1)S(1)}, bf16[256,1,128]{0,2,1:T(8,128)(2,1)S(1)}, u32[]{:S(2)}, u32[]{:S(2)}) collective-permute-start(bf16[256,1,128]{0,2,1:T(8,128)(2,1)S(1)} %get-tuple-element.257), channel_id=1, source_target_pairs={{1,0},{2,1},{3,2},{4,3},{5,4},{6,5},{7,6},{8,7},{9,8},{10,9},{11,1... | collective-permute-start | bytes 196616 | tf_op jit(solution)/shard_map/ppermute | solution.py:21
  21.6 1.7 copy-start.8
  24.2 5.3 %collective-permute-start.2 = (bf16[256,1,128]{0,2,1:T(8,128)(2,1)S(1)}, bf16[256,1,128]{0,2,1:T(8,128)(2,1)S(1)}, u32[]{:S(2)}, u32[]{:S(2)}) collective-permute-start(bf16[256,1,128]{0,2,1:T(8,128)(2,1)S(1)} %get-tuple-element.250), channel_id=1, source_target_pairs={{0,1},{1,2},{2,3},{3,4},{4,5},{5,6},{6,7},{7,8},{8,9},{9,10},{10,1... | collective-permute-start | bytes 196616 | tf_op jit(solution)/shard_map/ppermute | solution.py:18
  28.2 5.0 %collective-permute-start.3 = (bf16[256,1,128]{0,2,1:T(8,128)(2,1)S(1)}, bf16[256,1,128]{0,2,1:T(8,128)(2,1)S(1)}, u32[]{:S(2)}, u32[]{:S(2)}) collective-permute-start(bf16[256,1,128]{0,2,1:T(8,128)(2,1)S(1)} %get-tuple-element.249), channel_id=1, source_target_pairs={{1,0},{2,1},{3,2},{4,3},{5,4},{6,5},{7,6},{8,7},{9,8},{10,9},{11,1... | collective-permute-start | bytes 196616 | tf_op jit(solution)/shard_map/ppermute | solution.py:21
  33.6 1.9 copy-start.10
  34.0 1.4 copy-start.5
  35.4 3.3 %copy-start.2 = (f32[1,84,4,128]{3,2,1,0:T(4,128)S(1)}, f32[1,84,4,128]{3,2,1,0:T(4,128)}, u32[]{:S(2)}) copy-start(f32[1,84,4,128]{3,2,1,0:T(4,128)} %param.11) | copy-start | bytes 516100
  38.7 163.9 %copy-start.4 = (bf16[256,84]{0,1:T(8,128)(2,1)S(1)}, bf16[256,84]{0,1:T(8,128)(2,1)}, u32[]{:S(2)}) copy-start(bf16[256,84]{0,1:T(8,128)(2,1)} %param.13) | copy-start | bytes 129028
  38.7 163.9 %copy-start.7 = (f32[256]{0:T(256)S(1)}, f32[256]{0:T(256)}, u32[]{:S(2)}) copy-start(f32[256]{0:T(256)} %param.14) | copy-start | bytes 3076
  39.4 162.1 %all-reduce.2.cloned.1.call-start = ((), (), s32[]{:S(2)}) async-start(), calls=%async_computation.1 | async-start | bytes 344064 | tf_op jit(solution)/shard_map/psum | solution.py:40
  40.2 233.5 %all-gather.6.cloned.1.call-start = ((), (), s32[]{:S(2)}) async-start(), calls=%async_computation.2 | async-start | bytes 2924544 | tf_op jit(solution)/shard_map/all_gather | solution.py:28
  202.8 4.7 %collective-permute-start.4 = (bf16[256,1,128]{0,2,1:T(8,128)(2,1)S(1)}, bf16[256,1,128]{0,2,1:T(8,128)(2,1)S(1)}, u32[]{:S(2)}, u32[]{:S(2)}) collective-permute-start(bf16[256,1,128]{0,2,1:T(8,128)(2,1)S(1)} %get-tuple-element.242), channel_id=1, source_target_pairs={{0,1},{1,2},{2,3},{3,4},{4,5},{5,6},{6,7},{7,8},{8,9},{9,10},{10,1... | collective-permute-start | bytes 196616 | tf_op jit(solution)/shard_map/ppermute | solution.py:18
  206.0 5.4 %collective-permute-start.5 = (bf16[256,1,128]{0,2,1:T(8,128)(2,1)S(1)}, bf16[256,1,128]{0,2,1:T(8,128)(2,1)S(1)}, u32[]{:S(2)}, u32[]{:S(2)}) collective-permute-start(bf16[256,1,128]{0,2,1:T(8,128)(2,1)S(1)} %get-tuple-element.241), channel_id=1, source_target_pairs={{1,0},{2,1},{3,2},{4,3},{5,4},{6,5},{7,6},{8,7},{9,8},{10,9},{11,1... | collective-permute-start | bytes 196616 | tf_op jit(solution)/shard_map/ppermute | solution.py:21
  211.7 1.7 copy-start.9
  214.4 4.5 %collective-permute-start.6 = (bf16[256,1,128]{0,2,1:T(8,128)(2,1)S(1)}, bf16[256,1,128]{0,2,1:T(8,128)(2,1)S(1)}, u32[]{:S(2)}, u32[]{:S(2)}) collective-permute-start(bf16[256,1,128]{0,2,1:T(8,128)(2,1)S(1)} %get-tuple-element.234), channel_id=1, source_target_pairs={{0,1},{1,2},{2,3},{3,4},{4,5},{5,6},{6,7},{7,8},{8,9},{9,10},{10,1... | collective-permute-start | bytes 196616 | tf_op jit(solution)/shard_map/ppermute | solution.py:18
  217.5 6.0 %collective-permute-start.7 = (bf16[256,1,128]{0,2,1:T(8,128)(2,1)S(1)}, bf16[256,1,128]{0,2,1:T(8,128)(2,1)S(1)}, u32[]{:S(2)}, u32[]{:S(2)}) collective-permute-start(bf16[256,1,128]{0,2,1:T(8,128)(2,1)S(1)} %get-tuple-element.233), channel_id=1, source_target_pairs={{1,0},{2,1},{3,2},{4,3},{5,4},{6,5},{7,6},{8,7},{9,8},{10,9},{11,1... | collective-permute-start | bytes 196616 | tf_op jit(solution)/shard_map/ppermute | solution.py:21
  224.3 1.4 copy-start.6
  228.8 62.2 %copy-start.3 = (f32[84,4,128]{2,1,0:T(4,128)S(1)}, f32[84,4,128]{2,1,0:T(4,128)}, u32[]{:S(2)}) copy-start(f32[84,4,128]{2,1,0:T(4,128)} %all-reduce.2.cloned.1.call-done) | copy-start | bytes 516100
  229.6 61.4 %copy-start.1 = (f32[42,8,128]{2,1,0:T(8,128)S(1)}, f32[42,8,128]{2,1,0:T(8,128)}, u32[]{:S(2)}) copy-start(f32[42,8,128]{2,1,0:T(8,128)} %subtract_multiply_fusion) | copy-start | bytes 516100
Sparse Core Ops, SparseCore 0:
  39.6 51.8 all-gather.3
  93.8 107.6 all-reduce.1
  229.7 43.8 all-gather.5
where the time goes:
time: 300 us; the launch traced here: 298 us
  waiting for transfers between devices  201 us (67%)
  other arithmetic  42.8 us (14%)
  starting transfers between devices  19.5 us (6%)
  between operations  18.7 us (6%)
  matrix products  9.37 us (3%)
  local copies, waits for them, and re-layouts  6.55 us (2%)
    all_gather x2, waiting for transfers between devices, carried_in(): pieces = lax.all_gather(value, axis)  95.3 us
    psum x1, waiting for transfers between devices, from_root(): return lax.psum(jnp.where(mine, array, jnp.zeros_like(array)), axis)  92.6 us
    select_n x30, other arithmetic, hop(): return jnp.where(position < mine, longer, subtotal)  34.4 us
    ppermute x4, starting transfers between devices, extended(): lax.ppermute(lax.slice_in_dim(block, block.shape[dim] - width, None, axis...  14.2 us
    ppermute x4, waiting for transfers between devices, extended(): lax.ppermute(lax.slice_in_dim(block, 0, width, axis=dim), axis, backward)  12.2 us
    dot_general x2, matrix products, field_drift(): jnp.dot(out_weight, hidden_two.reshape(hidden_two.shape[0], -1), preferre...  6.29 us
  transfers between devices with their start and end apart: 11, of which 7 were waited for; matrix products, arithmetic and copies ran while one was open for 6% of the time, Pallas kernels for 0%

commit v1 on v0

--- a/solution.py
+++ b/solution.py
@@ -37,7 +37,7 @@
 
 def from_root(array, axis, root):
     mine = lax.axis_index(axis) == root
-    return lax.psum(jnp.where(mine, array, jnp.zeros_like(array)), axis)
+    return jnp.sum(lax.all_gather(jnp.where(mine, array, jnp.zeros_like(array)), axis), axis=0)
 
 
 def level_sigma(levels):

time: 300 us -> 226 us (0.75)
  waiting for transfers between devices: 201 us -> 127 us
    psum x1 -> x0, waiting for transfers between devices: 92.6 us -> none  [from_root(): return lax.psum(jnp.where(mine, array, jnp.zeros_like(array)), axis)]
    all_gather x0 -> x1, waiting for transfers between devices: none -> 29.2 us  [from_root(): lax.all_gather(jnp.where(mine, array, jnp.zeros_like(array)), axis)]
    all_gather x2, waiting for transfers between devices: 95.3 us -> 85.5 us  [carried_in(): pieces = lax.all_gather(value, axis)]
  transfers between devices with their start and end apart: 11 -> 11, of which waited for: 7 -> 6; matrix products, arithmetic and copies ran while one was open for 6% -> 4% of each run, Pallas kernels for 0% -> 0%
where the time goes in v1:
time: 226 us; the launch traced here: 225 us
  waiting for transfers between devices  127 us (56%)
  other arithmetic  44.1 us (20%)
  starting transfers between devices  19.6 us (9%)
  between operations  18.4 us (8%)
  matrix products  9.36 us (4%)
  local copies, waits for them, and re-layouts  6.57 us (3%)
    all_gather x2, waiting for transfers between devices, carried_in(): pieces = lax.all_gather(value, axis)  85.5 us
    select_n x30, other arithmetic, hop(): return jnp.where(position < mine, longer, subtotal)  34.4 us
    all_gather x1, waiting for transfers between devices, from_root(): lax.all_gather(jnp.where(mine, array, jnp.zeros_like(array)), axis)  29.2 us
    ppermute x4, starting transfers between devices, extended(): lax.ppermute(lax.slice_in_dim(block, block.shape[dim] - width, None, axis...  14.4 us
    ppermute x4, waiting for transfers between devices, extended(): lax.ppermute(lax.slice_in_dim(block, 0, width, axis=dim), axis, backward)  11.8 us
    dot_general x2, matrix products, field_drift(): jnp.dot(out_weight, hidden_two.reshape(hidden_two.shape[0], -1), preferre...  6.29 us
    unnamed x26, local copies, waits for them, and re-layouts  5.75 us
    ppermute x4, starting transfers between devices, extended(): lax.ppermute(lax.slice_in_dim(block, 0, width, axis=dim), axis, backward)  5.17 us
  transfers between devices with their start and end apart: 11, of which 6 were waited for; matrix products, arithmetic and copies ran while one was open for 4% of the time, Pallas kernels for 0%

profile of v1, /device:TPU:1, one launch (start us, length us, event | category | flops | bytes accessed | tf_op | source)
XLA Modules:
  0.0 225.0 jit_solution(14181750596278524803)
XLA Ops:
  9.3 1.6 broadcast_select_fusion
  12.0 4.0 %collective-permute-start = (bf16[256,1,128]{0,2,1:T(8,128)(2,1)S(1)}, bf16[256,1,128]{0,2,1:T(8,128)(2,1)S(1)}, u32[]{:S(2)}, u32[]{:S(2)}) collective-permute-start(bf16[256,1,128]{0,2,1:T(8,128)(2,1)S(1)} %get-tuple-element.258), channel_id=1, source_target_pairs={{0,1},{1,2},{2,3},{3,4},{4,5},{5,6},{6,7},{7,8},{8,9},{9,10},{10,1... | collective-permute-start | bytes 196616 | tf_op jit(solution)/shard_map/ppermute | solution.py:18
  16.1 1.3 collective-permute-start.1
  21.7 1.4 copy-done.7
  24.1 4.0 %collective-permute-start.2 = (bf16[256,1,128]{0,2,1:T(8,128)(2,1)S(1)}, bf16[256,1,128]{0,2,1:T(8,128)(2,1)S(1)}, u32[]{:S(2)}, u32[]{:S(2)}) collective-permute-start(bf16[256,1,128]{0,2,1:T(8,128)(2,1)S(1)} %get-tuple-element.250), channel_id=1, source_target_pairs={{0,1},{1,2},{2,3},{3,4},{4,5},{5,6},{6,7},{7,8},{8,9},{9,10},{10,1... | collective-permute-start | bytes 196616 | tf_op jit(solution)/shard_map/ppermute | solution.py:18
  28.1 1.3 collective-permute-start.3
  29.4 3.8 %collective-permute-done.3 = bf16[256,1,128]{0,2,1:T(8,128)(2,1)S(1)} collective-permute-done((bf16[256,1,128]{0,2,1:T(8,128)(2,1)S(1)}, bf16[256,1,128]{0,2,1:T(8,128)(2,1)S(1)}, u32[]{:S(2)}, u32[]{:S(2)}) %collective-permute-start.3) | collective-permute-done | bytes 65568 | tf_op jit(solution)/shard_map/ppermute | solution.py:21
  34.0 1.4 copy-done.4
  35.4 3.2 %fusion.13 = f32[84,512]{1,0:T(8,128)S(1)} fusion(bf16[84,256]{1,0:T(8,128)(2,1)S(1)} %copy-done.9, bf16[2304,512]{0,1:T(8,128)(2,1)} %bitcast.143, bf16[2,256,2304]{2,1,0:T(8,128)(2,1)} %param.15, f32[512,256]{1,0:T(8,128)S(1)} %fusion.10, f32[256]{0:T(256)S(1)} %get-tuple-element.264, f32[256]{0:T(256)S(1)} %get-tuple-element.263, ...), kind=kOutput, calls=%fused_computation.21 | convolution fusion | flops 628140032 | bytes 4282372 | tf_op jit(solution)/shard_map/dot_general | solution.py:102
  39.4 29.2 %all-gather.7.cloned.1.call-done = f32[16,84,4,128]{3,2,1,0:T(4,128)} async-done(((f32[1,84,4,128]{3,2,1,0:T(4,128)}), f32[16,84,4,128]{3,2,1,0:T(4,128)}) %all-gather.7.cloned.1.call-update) | async-done | bytes 2752528 | tf_op jit(solution)/shard_map/all_gather | solution.py:40
  68.6 2.2 reduce_sum.9
  70.8 41.6 %all-gather.5.cloned.1.call-done = f32[16,84,4,128]{3,2,1,0:T(4,128)} async-done(((f32[1,84,4,128]{3,2,1,0:T(4,128)}), f32[16,84,4,128]{3,2,1,0:T(4,128)}) %all-gather.5.cloned.1.call-update) | async-done | bytes 2752528 | tf_op jit(solution)/shard_map/all_gather | solution.py:28
  112.5 17.3 %while.28 = (s32[]{:T(128)}, f32[84,4,128]{2,1,0:T(4,128)S(1)}, s32[]{:T(128)}, f32[16,84,4,128]{3,2,1,0:T(4,128)}, s32[]{:T(128)}, /*index=5*/s32[]{:T(128)}) while((s32[]{:T(128)}, f32[84,4,128]{2,1,0:T(4,128)S(1)}, s32[]{:T(128)}, f32[16,84,4,128]{3,2,1,0:T(4,128)}, s32[]{:T(128)}, /*index=5*/s32[]{:T(128)}) %tuple.98), condition=%wide.region_1.2_spmd.clone, body=%wide.region_0.1_spmd.clone.sunk | while | flops 129028 | bytes 516189 | solution.py:35
  113.6 1.1 add_select_fusion.4
  114.8 1.1 add_select_fusion.4
  115.9 1.1 add_select_fusion.4
  117.1 1.1 add_select_fusion.4
  118.2 1.1 add_select_fusion.4
  119.4 1.1 add_select_fusion.4
  120.6 1.1 add_select_fusion.4
  121.7 1.1 add_select_fusion.4
  122.9 1.1 add_select_fusion.4
  124.0 1.1 add_select_fusion.4
  125.2 1.1 add_select_fusion.4
  126.3 1.1 add_select_fusion.4
  127.5 1.1 add_select_fusion.4
  128.7 1.1 add_select_fusion.4
  130.2 3.2 %collective-permute-start.4 = (bf16[256,1,128]{0,2,1:T(8,128)(2,1)S(1)}, bf16[256,1,128]{0,2,1:T(8,128)(2,1)S(1)}, u32[]{:S(2)}, u32[]{:S(2)}) collective-permute-start(bf16[256,1,128]{0,2,1:T(8,128)(2,1)S(1)} %get-tuple-element.242), channel_id=1, source_target_pairs={{0,1},{1,2},{2,3},{3,4},{4,5},{5,6},{6,7},{7,8},{8,9},{9,10},{10,1... | collective-permute-start | bytes 196616 | tf_op jit(solution)/shard_map/ppermute | solution.py:18
  133.5 1.3 collective-permute-start.5
  134.8 3.7 %collective-permute-done.5 = bf16[256,1,128]{0,2,1:T(8,128)(2,1)S(1)} collective-permute-done((bf16[256,1,128]{0,2,1:T(8,128)(2,1)S(1)}, bf16[256,1,128]{0,2,1:T(8,128)(2,1)S(1)}, u32[]{:S(2)}, u32[]{:S(2)}) %collective-permute-start.5) | collective-permute-done | bytes 65568 | tf_op jit(solution)/shard_map/ppermute | solution.py:21
  139.1 1.4 copy-done.8
  141.5 3.1 %collective-permute-start.6 = (bf16[256,1,128]{0,2,1:T(8,128)(2,1)S(1)}, bf16[256,1,128]{0,2,1:T(8,128)(2,1)S(1)}, u32[]{:S(2)}, u32[]{:S(2)}) collective-permute-start(bf16[256,1,128]{0,2,1:T(8,128)(2,1)S(1)} %get-tuple-element.234), channel_id=1, source_target_pairs={{0,1},{1,2},{2,3},{3,4},{4,5},{5,6},{6,7},{7,8},{8,9},{9,10},{10,1... | collective-permute-start | bytes 196616 | tf_op jit(solution)/shard_map/ppermute | solution.py:18
  144.6 1.3 collective-permute-start.7
  145.9 4.4 %collective-permute-done.7 = bf16[256,1,128]{0,2,1:T(8,128)(2,1)S(1)} collective-permute-done((bf16[256,1,128]{0,2,1:T(8,128)(2,1)S(1)}, bf16[256,1,128]{0,2,1:T(8,128)(2,1)S(1)}, u32[]{:S(2)}, u32[]{:S(2)}) %collective-permute-start.7) | collective-permute-done | bytes 65568 | tf_op jit(solution)/shard_map/ppermute | solution.py:21
  151.1 1.4 copy-done.5
  152.5 3.1 %fusion.12 = f32[84,512]{1,0:T(8,128)S(1)} fusion(bf16[84,256]{1,0:T(8,128)(2,1)S(1)} %copy-done.9, bf16[2304,512]{0,1:T(8,128)(2,1)} %bitcast.145, bf16[2,256,2304]{2,1,0:T(8,128)(2,1)} %param.15, f32[512,256]{1,0:T(8,128)S(1)} %fusion.8, f32[256]{0:T(256)S(1)} %get-tuple-element.264, f32[256]{0:T(256)S(1)} %get-tuple-element.263, ...), kind=kOutput, calls=%fused_computation.19 | convolution fusion | flops 628140032 | bytes 4282372 | tf_op jit(solution)/shard_map/dot_general | solution.py:102
  156.5 43.9 %all-gather.9.cloned.1.call-done = f32[1344,4,128]{2,1,0:T(4,128)} async-done(((f32[84,4,128]{2,1,0:T(4,128)}), f32[1344,4,128]{2,1,0:T(4,128)}) %all-gather.9.cloned.1.call-update) | async-done | bytes 2752528 | tf_op jit(solution)/shard_map/all_gather | solution.py:28
  200.3 17.3 %while.29 = (s32[]{:T(128)}, f32[84,4,128]{2,1,0:T(4,128)S(1)}, s32[]{:T(128)}, f32[16,84,4,128]{3,2,1,0:T(4,128)}, s32[]{:T(128)}, /*index=5*/s32[]{:T(128)}) while((s32[]{:T(128)}, f32[84,4,128]{2,1,0:T(4,128)S(1)}, s32[]{:T(128)}, f32[16,84,4,128]{3,2,1,0:T(4,128)}, s32[]{:T(128)}, /*index=5*/s32[]{:T(128)}) %tuple.110), condition=%wide.region_4.5_spmd.clone, body=%wide.region_3.4_spmd.clone.sunk | while | flops 129028 | bytes 516189 | solution.py:35
  201.5 1.1 add_select_fusion.5
  202.7 1.1 add_select_fusion.5
  203.8 1.1 add_select_fusion.5
  205.0 1.1 add_select_fusion.5
  206.1 1.1 add_select_fusion.5
  207.3 1.1 add_select_fusion.5
  208.4 1.1 add_select_fusion.5
  209.6 1.1 add_select_fusion.5
  210.8 1.1 add_select_fusion.5
  214.2 1.1 add_select_fusion.5
  (106 shorter events, 17.0 us)
Async XLA Ops:
  6.5 11.7 %copy-start = (bf16[256,1024]{1,0:T(8,128)(2,1)S(1)}, bf16[256,1024]{1,0:T(8,128)(2,1)}, u32[]{:S(2)}) copy-start(bf16[256,1024]{1,0:T(8,128)(2,1)} %param.16) | copy-start | bytes 1572868
  6.5 62.1 %all-gather.7.cloned.1.call-start = ((), (), s32[]{:S(2)}) async-start(), calls=%async_computation.1 | async-start | bytes 2924544 | tf_op jit(solution)/shard_map/all_gather | solution.py:40
  12.0 9.0 %collective-permute-start = (bf16[256,1,128]{0,2,1:T(8,128)(2,1)S(1)}, bf16[256,1,128]{0,2,1:T(8,128)(2,1)S(1)}, u32[]{:S(2)}, u32[]{:S(2)}) collective-permute-start(bf16[256,1,128]{0,2,1:T(8,128)(2,1)S(1)} %get-tuple-element.258), channel_id=1, source_target_pairs={{0,1},{1,2},{2,3},{3,4},{4,5},{5,6},{6,7},{7,8},{8,9},{9,10},{10,1... | collective-permute-start | bytes 196616 | tf_op jit(solution)/shard_map/ppermute | solution.py:18
  16.1 5.0 %collective-permute-start.1 = (bf16[256,1,128]{0,2,1:T(8,128)(2,1)S(1)}, bf16[256,1,128]{0,2,1:T(8,128)(2,1)S(1)}, u32[]{:S(2)}, u32[]{:S(2)}) collective-permute-start(bf16[256,1,128]{0,2,1:T(8,128)(2,1)S(1)} %get-tuple-element.257), channel_id=1, source_target_pairs={{1,0},{2,1},{3,2},{4,3},{5,4},{6,5},{7,6},{8,7},{9,8},{10,9},{11,1... | collective-permute-start | bytes 196616 | tf_op jit(solution)/shard_map/ppermute | solution.py:21
  17.4 95.1 %all-gather.5.cloned.1.call-start = ((), (), s32[]{:S(2)}) async-start(), calls=%async_computation | async-start | bytes 2924544 | tf_op jit(solution)/shard_map/all_gather | solution.py:28
  21.4 1.7 copy-start.7
  24.1 5.3 %collective-permute-start.2 = (bf16[256,1,128]{0,2,1:T(8,128)(2,1)S(1)}, bf16[256,1,128]{0,2,1:T(8,128)(2,1)S(1)}, u32[]{:S(2)}, u32[]{:S(2)}) collective-permute-start(bf16[256,1,128]{0,2,1:T(8,128)(2,1)S(1)} %get-tuple-element.250), channel_id=1, source_target_pairs={{0,1},{1,2},{2,3},{3,4},{4,5},{5,6},{6,7},{7,8},{8,9},{9,10},{10,1... | collective-permute-start | bytes 196616 | tf_op jit(solution)/shard_map/ppermute | solution.py:18
  28.1 5.1 %collective-permute-start.3 = (bf16[256,1,128]{0,2,1:T(8,128)(2,1)S(1)}, bf16[256,1,128]{0,2,1:T(8,128)(2,1)S(1)}, u32[]{:S(2)}, u32[]{:S(2)}) collective-permute-start(bf16[256,1,128]{0,2,1:T(8,128)(2,1)S(1)} %get-tuple-element.249), channel_id=1, source_target_pairs={{1,0},{2,1},{3,2},{4,3},{5,4},{6,5},{7,6},{8,7},{9,8},{10,9},{11,1... | collective-permute-start | bytes 196616 | tf_op jit(solution)/shard_map/ppermute | solution.py:21
  33.5 1.9 copy-start.9
  34.0 1.4 copy-start.4
  35.4 3.2 %copy-start.2 = (f32[1,84,4,128]{3,2,1,0:T(4,128)S(1)}, f32[1,84,4,128]{3,2,1,0:T(4,128)}, u32[]{:S(2)}) copy-start(f32[1,84,4,128]{3,2,1,0:T(4,128)} %param.11) | copy-start | bytes 516100
  39.4 161.0 %all-gather.9.cloned.1.call-start = ((), (), s32[]{:S(2)}) async-start(), calls=%async_computation.2 | async-start | bytes 2924544 | tf_op jit(solution)/shard_map/all_gather | solution.py:28
  70.8 59.1 %copy-start.3 = (bf16[256,84]{0,1:T(8,128)(2,1)S(1)}, bf16[256,84]{0,1:T(8,128)(2,1)}, u32[]{:S(2)}) copy-start(bf16[256,84]{0,1:T(8,128)(2,1)} %param.13) | copy-start | bytes 129028
  70.8 59.1 %copy-start.6 = (f32[256]{0:T(256)S(1)}, f32[256]{0:T(256)}, u32[]{:S(2)}) copy-start(f32[256]{0:T(256)} %param.14) | copy-start | bytes 3076
  130.2 4.6 %collective-permute-start.4 = (bf16[256,1,128]{0,2,1:T(8,128)(2,1)S(1)}, bf16[256,1,128]{0,2,1:T(8,128)(2,1)S(1)}, u32[]{:S(2)}, u32[]{:S(2)}) collective-permute-start(bf16[256,1,128]{0,2,1:T(8,128)(2,1)S(1)} %get-tuple-element.242), channel_id=1, source_target_pairs={{0,1},{1,2},{2,3},{3,4},{4,5},{5,6},{6,7},{7,8},{8,9},{9,10},{10,1... | collective-permute-start | bytes 196616 | tf_op jit(solution)/shard_map/ppermute | solution.py:18
  133.5 5.0 %collective-permute-start.5 = (bf16[256,1,128]{0,2,1:T(8,128)(2,1)S(1)}, bf16[256,1,128]{0,2,1:T(8,128)(2,1)S(1)}, u32[]{:S(2)}, u32[]{:S(2)}) collective-permute-start(bf16[256,1,128]{0,2,1:T(8,128)(2,1)S(1)} %get-tuple-element.241), channel_id=1, source_target_pairs={{1,0},{2,1},{3,2},{4,3},{5,4},{6,5},{7,6},{8,7},{9,8},{10,9},{11,1... | collective-permute-start | bytes 196616 | tf_op jit(solution)/shard_map/ppermute | solution.py:21
  138.8 1.7 copy-start.8
  141.5 4.4 %collective-permute-start.6 = (bf16[256,1,128]{0,2,1:T(8,128)(2,1)S(1)}, bf16[256,1,128]{0,2,1:T(8,128)(2,1)S(1)}, u32[]{:S(2)}, u32[]{:S(2)}) collective-permute-start(bf16[256,1,128]{0,2,1:T(8,128)(2,1)S(1)} %get-tuple-element.234), channel_id=1, source_target_pairs={{0,1},{1,2},{2,3},{3,4},{4,5},{5,6},{6,7},{7,8},{8,9},{9,10},{10,1... | collective-permute-start | bytes 196616 | tf_op jit(solution)/shard_map/ppermute | solution.py:18
  144.6 5.7 %collective-permute-start.7 = (bf16[256,1,128]{0,2,1:T(8,128)(2,1)S(1)}, bf16[256,1,128]{0,2,1:T(8,128)(2,1)S(1)}, u32[]{:S(2)}, u32[]{:S(2)}) collective-permute-start(bf16[256,1,128]{0,2,1:T(8,128)(2,1)S(1)} %get-tuple-element.233), channel_id=1, source_target_pairs={{1,0},{2,1},{3,2},{4,3},{5,4},{6,5},{7,6},{8,7},{9,8},{10,9},{11,1... | collective-permute-start | bytes 196616 | tf_op jit(solution)/shard_map/ppermute | solution.py:21
  151.1 1.4 copy-start.5
  156.4 61.3 %copy-start.1 = (f32[42,8,128]{2,1,0:T(8,128)S(1)}, f32[42,8,128]{2,1,0:T(8,128)}, u32[]{:S(2)}) copy-start(f32[42,8,128]{2,1,0:T(8,128)} %subtract_multiply_fusion) | copy-start | bytes 516100
Sparse Core Ops, SparseCore 0:
  17.5 51.0 all-gather.6
  70.7 41.6 all-gather.4
  156.6 43.7 all-gather.8
